TPU v7x, 256 devices: a whole 4x4x8 slice. The times are simulated.
256 devices in a mesh: outer: 32 (over z, x), inner: 8 (over y, core).
Axes of the slice: x: 4, y: 4, z: 8, core: 2. Of those that a mesh axis runs over, the one named last changes fastest.
Arguments:
- queries: bfloat16 [32768, 2048], P(('outer', 'inner')), may hold values from -5 to 5
- key_rows: bfloat16 [32768, 2048], P(('outer', 'inner')), may hold values from -5 to 5
- value_rows: bfloat16 [32768, 2048], P(('outer', 'inner')), may hold values from -6 to 6
- out_grad: bfloat16 [32768, 2048], P(('outer', 'inner')), may hold values from -6 to 6
- log_gate: float32 [16, 32768], P(None, ('outer', 'inner')), may hold values from -1 to 0
Outputs:
- mixed_out: bfloat16 [32768, 2048], P(('outer', 'inner'))
- query_grad: bfloat16 [32768, 2048], P(('outer', 'inner'))
- key_grad: bfloat16 [32768, 2048], P(('outer', 'inner'))
- value_grad: bfloat16 [32768, 2048], P(('outer', 'inner'))
All inputs are finite; a program needn't handle non-finite values.
Results may differ from a plain program's by a relative error of at most 0.007.
Values may be sent and summed in bfloat16 or wider, within the bound.
No kernel may reach another device: no remote copies, remote signals or barrier semaphores. Data moves between devices by JAX's collectives and lax.ppermute only.
A program may use at most 256 MiB of HBM per device.

v0:
```python
import jax
import jax.numpy as jnp
from jax import lax
from jax.sharding import PartitionSpec as P

W = 64


def from_behind(value, axis, steps):
    count = lax.axis_size(axis)
    first, last = (max(0, -steps), min(count, count - steps))
    return lax.ppermute(value, axis, [(source, source + steps) for source in range(first, last)])


def carried_in(part, axis, combine, identity, reverse):
    count = lax.axis_size(axis)
    place = lax.axis_index(axis)
    ahead = count - 1 - place if reverse else place
    gathered = jax.tree.map(lambda a: lax.all_gather(a, axis), part)
    state = jax.tree.map(lambda a, e: jnp.zeros_like(a) + jnp.asarray(e, a.dtype), part, identity)

    def one(hop, state):
        source = count - 1 - hop if reverse else hop
        return combine(
            state, jax.tree.map(lambda a: lax.dynamic_index_in_dim(a, source, 0, False), gathered)
        )

    return lax.fori_loop(0, ahead, one, state)


def low_product(form, left, right):
    return jnp.einsum(form, left, right, preferred_element_type=jnp.float32)


def high_product(form, left, right):
    return jnp.einsum(form, left, right, precision=lax.Precision.HIGHEST)


def local_states(query_blk, key_blk, value_blk, grad_blk, gate_rows):
    cumul_gate = jnp.cumsum(gate_rows, axis=1)
    last_cumul = cumul_gate[:, -1:]
    block_decay = jnp.exp(cumul_gate[:, -1])
    tail_weight = jnp.exp(last_cumul - cumul_gate).T
    head_weight = jnp.exp(cumul_gate).T
    state_local = high_product(
        "thf,the->hfe",
        key_blk.astype(jnp.float32) * tail_weight[:, :, None],
        value_blk.astype(jnp.float32),
    )
    grad_local = high_product(
        "thf,the->hfe",
        query_blk.astype(jnp.float32) * head_weight[:, :, None],
        grad_blk.astype(jnp.float32),
    )
    return (block_decay, state_local, grad_local)


def block_terms(
    query_blk,
    key_blk,
    value_blk,
    grad_blk,
    gate_rows,
    state_in,
    grad_after,
    key_halo,
    value_halo,
    halo_live,
    lin_scale,
):
    row_count = query_blk.shape[0]
    halo_rows = key_halo.shape[0]
    head_size = query_blk.shape[2]
    cumul_gate = jnp.cumsum(gate_rows, axis=1)
    last_cumul = cumul_gate[:, -1:]
    head_weight = jnp.exp(cumul_gate).T
    tail_weight = jnp.exp(last_cumul - cumul_gate).T
    query_pos = jnp.arange(row_count)[:, None]
    key_pos = jnp.arange(row_count)[None, :]
    causal_mask = (key_pos <= query_pos)[None]
    gap_logs = cumul_gate[:, :, None] - cumul_gate[:, None, :]
    decay_grid = jnp.where(causal_mask, jnp.exp(jnp.where(causal_mask, gap_logs, 0.0)), 0.0)
    lin_weight = (low_product("thf,shf->hts", query_blk, key_blk) * decay_grid).astype(jnp.bfloat16)
    query_decayed = query_blk.astype(jnp.float32) * head_weight[:, :, None]
    lin_out = low_product("hts,she->the", lin_weight, value_blk) + high_product(
        "thf,hfe->the", query_decayed, state_in
    )
    ext_keys = jnp.concatenate([key_halo, key_blk], axis=0)
    ext_values = jnp.concatenate([value_halo, value_blk], axis=0)
    ext_pos = jnp.arange(row_count + halo_rows)[None, :]
    in_band = (
        (ext_pos > query_pos)
        & (ext_pos <= query_pos + halo_rows)
        & ((ext_pos >= halo_rows) | halo_live)
    )[None]
    logits = low_product("thf,jhf->htj", query_blk, ext_keys) * head_size ** (-0.5)
    masked_logits = jnp.where(in_band, logits, -jnp.inf)
    row_max = jnp.max(masked_logits, axis=2, keepdims=True)
    expo_terms = jnp.exp(masked_logits - row_max)
    win_prob = expo_terms / jnp.sum(expo_terms, axis=2, keepdims=True)
    prob_low = win_prob.astype(jnp.bfloat16)
    win_out = low_product("htj,jhe->the", prob_low, ext_values)
    output = (lin_scale * lin_out + win_out).astype(jnp.bfloat16)
    grad_weight = (low_product("the,she->hts", grad_blk, value_blk) * decay_grid).astype(
        jnp.bfloat16
    )
    grad_decayed = grad_blk.astype(jnp.float32) * head_weight[:, :, None]
    query_lin = low_product("hts,shf->thf", grad_weight, key_blk) + high_product(
        "the,hfe->thf", grad_decayed, state_in
    )
    value_tail = value_blk.astype(jnp.float32) * tail_weight[:, :, None]
    key_tail = key_blk.astype(jnp.float32) * tail_weight[:, :, None]
    key_lin = low_product("hts,thf->shf", grad_weight, query_blk) + high_product(
        "she,hfe->shf", value_tail, grad_after
    )
    value_lin = low_product("hts,the->she", lin_weight, grad_blk) + high_product(
        "shf,hfe->she", key_tail, grad_after
    )
    prob_grad = low_product("the,jhe->htj", grad_blk, ext_values)
    row_delta = jnp.sum(win_prob * prob_grad, axis=2, keepdims=True)
    logit_grad = (win_prob * (prob_grad - row_delta) * head_size ** (-0.5)).astype(jnp.bfloat16)
    query_win = low_product("htj,jhf->thf", logit_grad, ext_keys)
    key_ext = low_product("htj,thf->jhf", logit_grad, query_blk)
    value_ext = low_product("htj,the->jhe", prob_low, grad_blk)
    query_grad = (lin_scale * query_lin + query_win).astype(jnp.bfloat16)
    key_local = lin_scale * key_lin + key_ext[halo_rows:]
    value_local = lin_scale * value_lin + value_ext[halo_rows:]
    return (output, query_grad, key_local, value_local, key_ext[:halo_rows], value_ext[:halo_rows])


def forward_merge(earlier_part, later_part):
    return (
        earlier_part[0] * later_part[0],
        later_part[0][:, None, None] * earlier_part[1] + later_part[1],
    )


def backward_merge(earlier_part, later_part):
    return (
        earlier_part[0] * later_part[0],
        later_part[1] + later_part[0][:, None, None] * earlier_part[1],
    )


def run_forward(running, element):
    return (forward_merge(running, element), running)


def run_backward(running, element):
    return (backward_merge(running, element), running)


def select_mine(bundle, inner_pos):
    return tuple(
        (lax.dynamic_index_in_dim(member, inner_pos, 0, keepdims=False) for member in bundle)
    )


def per_device(queries, key_rows, value_rows, out_grad, log_gate):
    row_count = queries.shape[0]
    head_count = log_gate.shape[0]
    head_size = queries.shape[1] // head_count
    devices = lax.axis_size("outer") * lax.axis_size("inner")
    lin_scale = (head_size * row_count * devices) ** (-0.5)
    block_shape = (row_count, head_count, head_size)
    query_blk = queries.reshape(block_shape)
    key_blk = key_rows.reshape(block_shape)
    value_blk = value_rows.reshape(block_shape)
    grad_blk = out_grad.reshape(block_shape)
    block_decay, state_local, grad_local = local_states(
        query_blk, key_blk, value_blk, grad_blk, log_gate
    )
    key_halo, value_halo = from_behind((key_blk[-W:], value_blk[-W:]), ("outer", "inner"), 1)
    position = lax.axis_index("outer") * lax.axis_size("inner") + lax.axis_index("inner")
    identity_pair = (
        jnp.ones((head_count,), jnp.float32),
        jnp.zeros((head_count, head_size, head_size), jnp.float32),
    )
    gathered = (
        lax.all_gather(block_decay[None], "inner", axis=0, tiled=True),
        lax.all_gather(state_local[None], "inner", axis=0, tiled=True),
        lax.all_gather(grad_local[None], "inner", axis=0, tiled=True),
    )
    group_decay, group_state, group_grad = gathered
    total_forward, before_forward = lax.scan(run_forward, identity_pair, (group_decay, group_state))
    total_backward, after_backward = lax.scan(
        run_backward, identity_pair, (group_decay, group_grad), reverse=True
    )
    inner_pos = lax.axis_index("inner")
    mine_forward = select_mine(before_forward, inner_pos)
    mine_backward = select_mine(after_backward, inner_pos)
    outer_forward = carried_in(total_forward, "outer", forward_merge, identity_pair, False)
    outer_backward = carried_in(total_backward, "outer", backward_merge, identity_pair, True)
    forward_pair = forward_merge(outer_forward, mine_forward)
    backward_pair = backward_merge(outer_backward, mine_backward)
    output, query_grad, key_local, value_local, key_back, value_back = block_terms(
        query_blk,
        key_blk,
        value_blk,
        grad_blk,
        log_gate,
        forward_pair[1],
        backward_pair[1],
        key_halo,
        value_halo,
        position > 0,
        lin_scale,
    )
    key_return, value_return = (
        from_behind(key_back.astype(jnp.bfloat16), ("outer", "inner"), -1).astype(key_back.dtype),
        from_behind(value_back.astype(jnp.bfloat16), ("outer", "inner"), -1).astype(
            value_back.dtype
        ),
    )
    key_grad = key_local.at[-W:].add(key_return).astype(jnp.bfloat16)
    value_grad = value_local.at[-W:].add(value_return).astype(jnp.bfloat16)
    flat_shape = (row_count, head_count * head_size)
    return (
        output.reshape(flat_shape),
        query_grad.reshape(flat_shape),
        key_grad.reshape(flat_shape),
        value_grad.reshape(flat_shape),
    )


def solution(mesh):
    placed = (
        P(("outer", "inner"), None),
        P(("outer", "inner"), None),
        P(("outer", "inner"), None),
        P(("outer", "inner"), None),
        P(None, ("outer", "inner")),
    )
    return jax.shard_map(
        per_device,
        mesh=mesh,
        in_specs=placed,
        out_specs=(
            P(("outer", "inner"), None),
            P(("outer", "inner"), None),
            P(("outer", "inner"), None),
            P(("outer", "inner"), None),
        ),
        check_vma=False,
    )
```

profile of v0, /device:TPU:230, one launch (start us, length us, event | category | flops | bytes accessed | tf_op | source)
XLA Modules:
  0.0 660.7 jit_solution(8102679605573216670)
XLA Ops:
  11.1 2.2 fusion.33
  14.6 2.2 fusion.34
  18.4 15.5 %all-reduce = f32[128]{0:T(128)S(1)} all-reduce(f32[128]{0:T(128)S(1)} %dynamic-update-slice.6), channel_id=2, replica_groups=mesh['outer'=32,'inner'=8] {'inner'}, use_global_device_ids=true, to_apply=%add | all-reduce | flops 128 | bytes 1024
  34.0 32.2 %all-gather.16.cloned.1.call-done = f32[128,128,128]{2,1,0:T(8,128)} async-done(((f32[16,128,128]{2,1,0:T(8,128)}), f32[128,128,128]{2,1,0:T(8,128)}) %all-gather.16.cloned.1.call-update) | async-done | bytes 8388624 | tf_op jit(solution)/shard_map/all_gather | solution.py:182
  66.1 4.4 broadcast.104.clone.1
  70.5 21.0 %while.69 = (s32[]{:T(128)}, f32[16]{0:T(128)S(1)}, f32[16,128,128]{2,1,0:T(8,128)S(1)}, f32[8,16]{1,0:T(8,128)S(1)}, f32[8,16,128,128]{3,2,1,0:T(8,128)}, /*ind...) while((s32[]{:T(128)}, f32[16]{0:T(128)S(1)}, ...), condition=%wide.region_9.10_spmd.clone, body=%wide.region_8.9_spmd.clone.sunk | while | flops 1048612 | bytes 5243533 | solution.py:186
  92.6 27.8 %all-gather.12.cloned.1.call-done = f32[128,128,128]{2,1,0:T(8,128)} async-done(((f32[16,128,128]{2,1,0:T(8,128)}), f32[128,128,128]{2,1,0:T(8,128)}) %all-gather.12.cloned.1.call-update) | async-done | bytes 8388624 | tf_op jit(solution)/shard_map/all_gather | solution.py:181
  120.4 4.3 broadcast.104.clone
  124.7 20.6 %while.68 = (s32[]{:T(128)}, f32[16]{0:T(128)S(1)}, f32[16,128,128]{2,1,0:T(8,128)S(1)}, f32[8,16]{1,0:T(8,128)S(1)}, f32[8,16,128,128]{3,2,1,0:T(8,128)}, /*ind...) while((s32[]{:T(128)}, f32[16]{0:T(128)S(1)}, ...), condition=%wide.region_2.3_spmd.clone, body=%wide.region_1.2_spmd.clone.sunk | while | flops 1048611 | bytes 5244021 | solution.py:185
  148.0 2.2 collective-permute-start.1
  151.2 2.5 collective-permute-start
  160.0 2.6 collective-permute-done.1
  162.6 2.7 fusion.70
  165.3 3.3 convolution_bitcast_fusion
  168.6 2.2 slice.107
  170.8 2.5 collective-permute-start.3
  173.3 2.5 fusion.44
  175.8 4.8 convolution_bitcast_fusion.1
  182.8 2.1 collective-permute-start.2
  185.4 72.2 %all-reduce.3 = (f32[512]{0:T(512)S(1)}, f32[512]{0:T(512)S(1)}) all-reduce(f32[512]{0:T(512)S(1)} %dynamic-update-slice.7, f32[512]{0:T(512)S(1)} %dynamic-update-slice.8), channel_id=4, replica_groups=mesh['outer'=32,'inner'=8] {'outer'}, use_global_device_ids=true, to_apply=%add.1 | all-reduce | flops 1024 | bytes 8192
  257.7 100.4 %all-gather.18.cloned.1.call-done = f32[512,128,128]{2,1,0:T(8,128)} async-done(((f32[16,128,128]{2,1,0:T(8,128)}), f32[512,128,128]{2,1,0:T(8,128)}) %all-gather.18.cloned.1.call-update) | async-done | bytes 33554448 | tf_op jit(solution)/shard_map/all_gather | solution.py:19
  358.5 3.3 convolution_bitcast_fusion.4
  363.3 2.4 slice_add_fusion
  365.6 7.0 %scatter-add.9 = f32[128,16,128]{0,2,1:T(8,128)} dynamic-update-slice(f32[128,16,128]{0,2,1:T(8,128)} %copy-done.2, f32[64,16,128]{0,2,1:T(8,128)} %slice_add_fusion, s32[]{:T(128)} %constant.187.clone.1, s32[]{:T(128)} %constant.180.clone.1, s32[]{:T(128)} %constant.180.clone.1) | dynamic-update-slice | bytes 1048580 | tf_op jit(solution)/shard_map/scatter-add | solution.py:216
  375.1 2.8 convolution_bitcast_fusion.5
  379.7 5.1 scatter-add.6
  385.9 204.5 %all-gather.14.cloned.1.call-done = f32[512,128,128]{2,1,0:T(8,128)} async-done(((f32[16,128,128]{2,1,0:T(8,128)}), f32[512,128,128]{2,1,0:T(8,128)}) %all-gather.14.cloned.1.call-update) | async-done | bytes 33554448 | tf_op jit(solution)/shard_map/all_gather | solution.py:19
  590.6 46.6 %while.66 = (s32[]{:T(128)}, f32[16,128,128]{2,1,0:T(8,128)S(1)}, s32[]{:T(128)}, f32[32,16]{1,0:T(8,128)S(1)}, f32[32,16,128,128]{3,2,1,0:T(8,128)}, /*index=5*/s32[]{:T(128)}, s32[]{:T(128)}, s32[]{:T(128)}) while((s32[]{:T(128)}, f32[16,128,128]{2,1,0:T(8,128)S(1)}, s32[]{:T(128)}, f32[32,16]{1,0:T(8,128)S(1)}, ...), condition=%wide.region_4.5_spmd, body=%wide.region_3.4_spmd.sunk | while | flops 524293 | bytes 3146047 | solution.py:28
  637.1 3.6 fusion.20
  640.7 4.3 fusion.26
  646.5 4.2 fusion.22
  650.7 2.5 fusion.25
  (224 shorter events, 115.3 us)
Async XLA Ops:
  7.2 59.0 %all-gather.16.cloned.1.call-start = ((), (), s32[]{:S(2)}) async-start(), calls=%async_computation.2 | async-start | bytes 9437184 | tf_op jit(solution)/shard_map/all_gather | solution.py:182
  11.1 2.3 copy-start.11
  13.3 1.0 copy-start.12
  13.3 107.1 %all-gather.12.cloned.1.call-start = ((), (), s32[]{:S(2)}) async-start(), calls=%async_computation | async-start | bytes 9437184 | tf_op jit(solution)/shard_map/all_gather | solution.py:181
  14.6 2.3 copy-start.17
  16.8 341.3 %all-gather.18.cloned.1.call-start = ((), (), s32[]{:S(2)}) async-start(), calls=%async_computation.3 | async-start | bytes 34603008 | tf_op jit(solution)/shard_map/all_gather | solution.py:19
  91.5 1.0 copy-start
  92.5 498.0 %all-gather.14.cloned.1.call-start = ((), (), s32[]{:S(2)}) async-start(), calls=%async_computation.1 | async-start | bytes 34603008 | tf_op jit(solution)/shard_map/all_gather | solution.py:19
  145.3 1.0 copy-start.1
  146.3 8.1 %copy-start.16 = (u32[256]{0:T(256)S(1)}, u32[256]{0:T(256)}, u32[]{:S(2)}) copy-start(u32[256]{0:T(256)} %constant.203) | copy-start | bytes 3076
  148.0 14.6 %collective-permute-start.1 = (bf16[64,16,128]{2,0,1:T(8,128)(2,1)}, bf16[64,16,128]{2,0,1:T(8,128)(2,1)}, u32[]{:S(2)}, u32[]{:S(2)}) collective-permute-start(bf16[64,16,128]{2,0,1:T(8,128)(2,1)} %copy_bitcast_fusion), channel_id=1, source_target_pairs={{0,1},{1,2},{2,3},{3,4},{4,5},{5,6},{6,7},{7,8},{8,9},{9,10},{10,1... | collective-permute-start | bytes 786440 | tf_op jit(solution)/shard_map/ppermute | solution.py:12
  151.2 22.1 %collective-permute-start = (bf16[64,16,128]{2,0,1:T(8,128)(2,1)S(1)}, bf16[64,16,128]{2,0,1:T(8,128)(2,1)}, u32[]{:S(2)}, u32[]{:S(2)}) collective-permute-start(bf16[64,16,128]{2,0,1:T(8,128)(2,1)S(1)} %copy_bitcast_fusion.1), channel_id=1, source_target_pairs={{0,1},{1,2},{2,3},{3,4},{4,5},{5,6},{6,7},{7,8},{8,9},{9,10},{10,1... | collective-permute-start | bytes 786440 | tf_op jit(solution)/shard_map/ppermute | solution.py:12
  154.0 11.2 %copy-start.15 = (bf16[128,16,128]{2,0,1:T(8,128)(2,1)}, bf16[128,16,128]{2,0,1:T(8,128)(2,1)S(1)}, u32[]{:S(2)}) copy-start(bf16[128,16,128]{2,0,1:T(8,128)(2,1)S(1)} %copy.84) | copy-start | bytes 1572868
  154.3 19.0 %copy-start.5 = (bf16[128,16,128]{2,0,1:T(8,128)(2,1)}, bf16[128,16,128]{2,0,1:T(8,128)(2,1)S(1)}, u32[]{:S(2)}) copy-start(bf16[128,16,128]{2,0,1:T(8,128)(2,1)S(1)} %copy.82) | copy-start | bytes 1572868
  156.4 2.1 copy-start.9
  157.0 3.0 copy-start.7
  170.8 191.5 %collective-permute-start.3 = (bf16[64,16,128]{0,2,1:T(8,128)(2,1)}, bf16[64,16,128]{0,2,1:T(8,128)(2,1)}, u32[]{:S(2)}, u32[]{:S(2)}) collective-permute-start(bf16[64,16,128]{0,2,1:T(8,128)(2,1)} %slice.107), channel_id=1, source_target_pairs={{1,0},{2,1},{3,2},{4,3},{5,4},{6,5},{7,6},{8,7},{9,8},{10,9},{11,1... | collective-permute-start | bytes 786440 | tf_op jit(solution)/shard_map/ppermute | solution.py:12
  182.8 195.6 %collective-permute-start.2 = (bf16[64,16,128]{0,2,1:T(8,128)(2,1)}, bf16[64,16,128]{0,2,1:T(8,128)(2,1)}, u32[]{:S(2)}, u32[]{:S(2)}) collective-permute-start(bf16[64,16,128]{0,2,1:T(8,128)(2,1)} %slice.108), channel_id=1, source_target_pairs={{1,0},{2,1},{3,2},{4,3},{5,4},{6,5},{7,6},{8,7},{9,8},{10,9},{11,1... | collective-permute-start | bytes 786440 | tf_op jit(solution)/shard_map/ppermute | solution.py:12
  358.5 3.4 copy-start.10
  358.5 3.4 copy-start.14
  362.3 1.0 copy-start.2
  375.1 2.8 copy-start.8
  375.1 2.8 copy-start.13
  590.6 46.6 %copy-start.4 = (f32[128,16,128]{0,2,1:T(8,128)S(1)}, f32[128,16,128]{0,2,1:T(8,128)}, u32[]{:S(2)}) copy-start(f32[128,16,128]{0,2,1:T(8,128)} %convolution_bitcast_fusion.7) | copy-start | bytes 3145732
  645.0 1.4 copy-start.3
  646.5 4.2 copy-start.6
Sparse Core Ops, SparseCore 0:
  13.5 52.6 all-gather.15
  68.0 52.3 all-gather.11
  123.0 235.1 all-gather.17
  360.6 229.8 all-gather.13
where the time goes:
time: 664 us; the launch traced here: 661 us
  waiting for transfers between devices  368 us (55%)
  other arithmetic  92.1 us (14%)
  blocking collectives  87.6 us (13%)
  matrix products  43.3 us (7%)
  local copies, waits for them, and re-layouts  43.1 us (6%)
  between operations  15.6 us (2%)
  starting transfers between devices  9.56 us (1%)
    all_gather x2, waiting for transfers between devices, carried_in(): gathered = jax.tree.map(lambda a: lax.all_gather(a, axis), part)  305 us
    unnamed x2, blocking collectives  87.6 us
    add x39, other arithmetic, forward_merge(): later_part[0][:, None, None] * earlier_part[1] + later_part[1]  56.4 us
    all_gather x1, waiting for transfers between devices, per_device(): lax.all_gather(grad_local[None], 'inner', axis=0, tiled=True)  32.2 us
    all_gather x1, waiting for transfers between devices, per_device(): lax.all_gather(state_local[None], 'inner', axis=0, tiled=True)  27.8 us
    dot_general x11, matrix products, low_product(): return jnp.einsum(form, left, right, preferred_element_type=jnp.float32)  22.3 us
    dot_general x6, matrix products, high_product(): return jnp.einsum(form, left, right, precision=lax.Precision.HIGHEST)  18.3 us
    dynamic_update_slice x16, other arithmetic, per_device(): lax.scan(run_forward, identity_pair, (group_decay, group_state))  17.3 us
  transfers between devices with their start and end apart: 8, of which 5 were waited for; matrix products, arithmetic and copies ran while one was open for 16% of the time, Pallas kernels for 0%

commit v1 on v0

--- a/solution.py
+++ b/solution.py
@@ -4,6 +4,38 @@
 from jax.sharding import PartitionSpec as P
 
 W = 64
+
+
+def refer_lots_all(base_x, dim_k):
+    mesh_name = "inner"
+    g_now = lax.axis_size(mesh_name)
+    q_next = lax.axis_index(mesh_name)
+    far_arr, heard, even = (g_now, q_next, base_x.shape[dim_k])
+    mixed_arr = range(far_arr)
+    later = map(lambda b: (b, (b + 1) % far_arr), mixed_arr)
+    shelf = list(later)
+    outer = range(far_arr)
+    then = map(lambda b: (b, (b - 1) % far_arr), outer)
+    sides = list(then)
+    local_out = jnp.zeros(
+        (*base_x.shape[:dim_k], far_arr * even, *base_x.shape[dim_k + 1 :]), base_x.dtype
+    )
+    local_out = lax.dynamic_update_slice_in_dim(local_out, base_x, heard * even, axis=dim_k)
+    a_next = plain = base_x
+    k_now = far_arr // 2
+    t = 1
+    while t < k_now + 1:
+        a_next = lax.ppermute(a_next, mesh_name, shelf)
+        local_out = lax.dynamic_update_slice_in_dim(
+            local_out, a_next, (heard - t) % far_arr * even, axis=dim_k
+        )
+        if t < far_arr - k_now:
+            plain = lax.ppermute(plain, mesh_name, sides)
+            local_out = lax.dynamic_update_slice_in_dim(
+                local_out, plain, (heard + t) % far_arr * even, axis=dim_k
+            )
+        t = t + 1
+    return local_out
 
 
 def from_behind(value, axis, steps):
@@ -178,7 +210,7 @@
     )
     gathered = (
         lax.all_gather(block_decay[None], "inner", axis=0, tiled=True),
-        lax.all_gather(state_local[None], "inner", axis=0, tiled=True),
+        refer_lots_all(state_local[None], 0),
         lax.all_gather(grad_local[None], "inner", axis=0, tiled=True),
     )
     group_decay, group_state, group_grad = gathered

time: 664 us -> 718 us (1.081)
  the two profiles are of different devices: /device:TPU:230 before, /device:TPU:1 now
where the time goes in v1:
time: 718 us; the launch traced here: 715 us
  waiting for transfers between devices  376 us (52%)
  blocking collectives  91.3 us (13%)
  other arithmetic  90.8 us (13%)
  local copies, waits for them, and re-layouts  62.3 us (9%)
  matrix products  47.6 us (7%)
  starting transfers between devices  29.4 us (4%)
  between operations  15.4 us (2%)
    all_gather x2, waiting for transfers between devices, carried_in(): gathered = jax.tree.map(lambda a: lax.all_gather(a, axis), part)  321 us
    unnamed x2, blocking collectives  91.3 us
    add x39, other arithmetic, backward_merge(): later_part[1] + later_part[0][:, None, None] * earlier_part[1]  56.5 us
    ppermute x4, waiting for transfers between devices, refer_lots_all(): a_next = lax.ppermute(a_next, mesh_name, shelf)  54.7 us
    dot_general x11, matrix products, low_product(): return jnp.einsum(form, left, right, preferred_element_type=jnp.float32)  25 us
    dot_general x6, matrix products, high_product(): return jnp.einsum(form, left, right, precision=lax.Precision.HIGHEST)  19.9 us
    dynamic_update_slice x16, other arithmetic, per_device(): lax.scan(run_forward, identity_pair, (group_decay, group_state))  17.3 us
  transfers between devices with their start and end apart: 14, of which 6 were waited for; matrix products, arithmetic and copies ran while one was open for 26% of the time, Pallas kernels for 0%

profile of v1, /device:TPU:1, one launch (start us, length us, event | category | flops | bytes accessed | tf_op | source)
XLA Modules:
  0.0 714.9 jit_solution(8747434265890142447)
XLA Ops:
  14.6 4.3 broadcast.111.clone.1
  21.1 2.7 collective-permute-start
  24.4 20.0 %collective-permute-done = f32[1,16,128,128]{3,2,1,0:T(8,128)S(1)} collective-permute-done((f32[1,16,128,128]{3,2,1,0:T(8,128)S(1)}, f32[1,16,128,128]{3,2,1,0:T(8,128)S(1)}, u32[]{:S(2)}, u32[]{:S(2)}) %collective-permute-start) | collective-permute-done | bytes 1048608 | tf_op jit(solution)/shard_map/ppermute | solution.py:28
  45.4 2.5 collective-permute-start.2
  47.9 6.9 collective-permute-start.3
  54.8 25.7 %collective-permute-done.2 = f32[1,16,128,128]{3,2,1,0:T(8,128)S(1)} collective-permute-done((f32[1,16,128,128]{3,2,1,0:T(8,128)S(1)}, f32[1,16,128,128]{3,2,1,0:T(8,128)S(1)}, u32[]{:S(2)}, u32[]{:S(2)}) %collective-permute-start.2) | collective-permute-done | bytes 1048608 | tf_op jit(solution)/shard_map/ppermute | solution.py:28
  80.5 2.5 collective-permute-start.4
  83.2 2.5 collective-permute-start.5
  85.8 8.9 %collective-permute-done.4 = f32[1,16,128,128]{3,2,1,0:T(8,128)} collective-permute-done((f32[1,16,128,128]{3,2,1,0:T(8,128)S(1)}, f32[1,16,128,128]{3,2,1,0:T(8,128)}, u32[]{:S(2)}, u32[]{:S(2)}) %collective-permute-start.4) | collective-permute-done | bytes 1048608 | tf_op jit(solution)/shard_map/ppermute | solution.py:28
  94.7 2.6 collective-permute-start.6
  98.8 23.5 %all-reduce = f32[128]{0:T(128)S(1)} all-reduce(f32[128]{0:T(128)S(1)} %dynamic-update-slice.6), channel_id=2, replica_groups=mesh['outer'=32,'inner'=8] {'inner'}, use_global_device_ids=true, to_apply=%add | all-reduce | flops 128 | bytes 1024
  122.4 2.5 constant_dynamic-update-slice_fusion.6
  136.8 4.3 broadcast.111.clone
  141.1 20.5 %while.68 = (s32[]{:T(128)}, f32[16]{0:T(128)S(1)}, f32[16,128,128]{2,1,0:T(8,128)S(1)}, f32[8,16]{1,0:T(8,128)S(1)}, f32[8,16,128,128]{3,2,1,0:T(8,128)}, /*ind...) while((s32[]{:T(128)}, f32[16]{0:T(128)S(1)}, ...), condition=%wide.region_2.3_spmd.clone, body=%wide.region_1.2_spmd.clone.sunk | while | flops 1048611 | bytes 5244021 | solution.py:217
  162.8 4.4 broadcast.111.clone.2
  167.1 20.9 %while.69 = (s32[]{:T(128)}, f32[16]{0:T(128)S(1)}, f32[16,128,128]{2,1,0:T(8,128)S(1)}, f32[8,16]{1,0:T(8,128)S(1)}, f32[8,16,128,128]{3,2,1,0:T(8,128)}, /*ind...) while((s32[]{:T(128)}, f32[16]{0:T(128)S(1)}, ...), condition=%wide.region_9.10_spmd.clone, body=%wide.region_8.9_spmd.clone.sunk | while | flops 1048612 | bytes 5243533 | solution.py:218
  201.7 2.7 fusion.69
  204.4 3.3 convolution_bitcast_fusion
  209.9 3.2 collective-permute-start.10
  215.6 4.9 convolution_bitcast_fusion.1
  225.2 67.8 %all-reduce.3 = (f32[512]{0:T(512)S(1)}, f32[512]{0:T(512)S(1)}) all-reduce(f32[512]{0:T(512)S(1)} %dynamic-update-slice.7, f32[512]{0:T(512)S(1)} %dynamic-update-slice.8), channel_id=3, replica_groups=mesh['outer'=32,'inner'=8] {'outer'}, use_global_device_ids=true, to_apply=%add.1 | all-reduce | flops 1024 | bytes 8192
  293.1 106.8 %all-gather.10.cloned.1.call-done = f32[512,128,128]{2,1,0:T(8,128)} async-done(((f32[16,128,128]{2,1,0:T(8,128)}), f32[512,128,128]{2,1,0:T(8,128)}) %all-gather.10.cloned.1.call-update) | async-done | bytes 33554448 | tf_op jit(solution)/shard_map/all_gather | solution.py:51
  400.1 3.8 fusion.20
  403.9 5.1 fusion.26
  411.0 4.5 fusion.22
  415.4 2.9 fusion.25
  419.4 214.4 %all-gather.14.cloned.1.call-done = f32[512,128,128]{2,1,0:T(8,128)} async-done(((f32[16,128,128]{2,1,0:T(8,128)}), f32[512,128,128]{2,1,0:T(8,128)}) %all-gather.14.cloned.1.call-update) | async-done | bytes 33554448 | tf_op jit(solution)/shard_map/all_gather | solution.py:51
  633.9 46.6 %while.67 = (s32[]{:T(128)}, f32[16,128,128]{2,1,0:T(8,128)S(1)}, s32[]{:T(128)}, f32[32,16,128,128]{3,2,1,0:T(8,128)}, f32[32,16]{1,0:T(8,128)S(1)}, /*index=5*/s32[]{:T(128)}, s32[]{:T(128)}, s32[]{:T(128)}, s32[]{:T(128)}) while((s32[]{:T(128)}, f32[16,128,128]{2,1,0:T(8,128)S(1)}, s32[]{:T(128)}, f32[32,16,128,128]{3,2,1,0:T(8,128)}, ...), condition=%wide.region_11.12_spmd, body=%wide.region_10.11_spmd.sunk | while | flops 524294 | bytes 3146067 | solution.py:60
  680.6 3.3 convolution_bitcast_fusion.4
  684.4 3.9 convolution_bitcast_fusion.5
  689.6 6.7 scatter-add.9
  702.2 5.1 scatter-add.6
  (247 shorter events, 146.1 us)
Async XLA Ops:
  7.2 155.6 %all-gather.12.cloned.1.call-start = ((), (), s32[]{:S(2)}) async-start(), calls=%async_computation.1 | async-start | bytes 9437184 | tf_op jit(solution)/shard_map/all_gather | solution.py:214
  11.1 2.3 copy-start.9
  13.3 1.0 copy-start.10
  13.3 386.6 %all-gather.10.cloned.1.call-start = ((), (), s32[]{:S(2)}) async-start(), calls=%async_computation | async-start | bytes 34603008 | tf_op jit(solution)/shard_map/all_gather | solution.py:51
  18.9 78.4 %copy-start.19 = (u32[256]{0:T(256)S(1)}, u32[256]{0:T(256)}, u32[]{:S(2)}) copy-start(u32[256]{0:T(256)} %constant.247) | copy-start | bytes 3076
  21.1 23.3 %collective-permute-start = (f32[1,16,128,128]{3,2,1,0:T(8,128)S(1)}, f32[1,16,128,128]{3,2,1,0:T(8,128)S(1)}, u32[]{:S(2)}, u32[]{:S(2)}) collective-permute-start(f32[1,16,128,128]{3,2,1,0:T(8,128)S(1)} %get-tuple-element.471), channel_id=1, source_target_pairs={{0,1},{1,2},{2,3},{3,4},{4,5},{5,6},{6,7},{7,0},{8,9},{9,10},{10,1... | collective-permute-start | bytes 3145736 | tf_op jit(solution)/shard_map/ppermute | solution.py:28
  23.8 24.1 %collective-permute-start.1 = (f32[1,16,128,128]{3,2,1,0:T(8,128)S(1)}, f32[1,16,128,128]{3,2,1,0:T(8,128)S(1)}, u32[]{:S(2)}, u32[]{:S(2)}) collective-permute-start(f32[1,16,128,128]{3,2,1,0:T(8,128)S(1)} %get-tuple-element.471), channel_id=1, source_target_pairs={{0,7},{1,0},{2,1},{3,2},{4,3},{5,4},{6,5},{7,6},{8,15},{9,8},{10,9... | collective-permute-start | bytes 3145736 | tf_op jit(solution)/shard_map/ppermute | solution.py:33
  45.4 35.1 %collective-permute-start.2 = (f32[1,16,128,128]{3,2,1,0:T(8,128)S(1)}, f32[1,16,128,128]{3,2,1,0:T(8,128)S(1)}, u32[]{:S(2)}, u32[]{:S(2)}) collective-permute-start(f32[1,16,128,128]{3,2,1,0:T(8,128)S(1)} %collective-permute-done), channel_id=1, source_target_pairs={{0,1},{1,2},{2,3},{3,4},{4,5},{5,6},{6,7},{7,0},{8,9},{9,10},{10,1... | collective-permute-start | bytes 3145736 | tf_op jit(solution)/shard_map/ppermute | solution.py:28
  47.9 32.6 %copy-start.13 = (f32[1,16,128,128]{3,2,1,0:T(8,128)}, f32[1,16,128,128]{3,2,1,0:T(8,128)S(1)}, u32[]{:S(2)}) copy-start(f32[1,16,128,128]{3,2,1,0:T(8,128)S(1)} %collective-permute-done.1) | copy-start | bytes 3145732
  47.9 35.4 %collective-permute-start.3 = (f32[1,16,128,128]{3,2,1,0:T(8,128)S(1)}, f32[1,16,128,128]{3,2,1,0:T(8,128)}, u32[]{:S(2)}, u32[]{:S(2)}) collective-permute-start(f32[1,16,128,128]{3,2,1,0:T(8,128)S(1)} %collective-permute-done.1), channel_id=1, source_target_pairs={{0,7},{1,0},{2,1},{3,2},{4,3},{5,4},{6,5},{7,6},{8,15},{9,8},{10,9... | collective-permute-start | bytes 3145736 | tf_op jit(solution)/shard_map/ppermute | solution.py:33
  80.5 2.8 copy-start.15
  80.5 14.2 %collective-permute-start.4 = (f32[1,16,128,128]{3,2,1,0:T(8,128)S(1)}, f32[1,16,128,128]{3,2,1,0:T(8,128)}, u32[]{:S(2)}, u32[]{:S(2)}) collective-permute-start(f32[1,16,128,128]{3,2,1,0:T(8,128)S(1)} %collective-permute-done.2), channel_id=1, source_target_pairs={{0,1},{1,2},{2,3},{3,4},{4,5},{5,6},{6,7},{7,0},{8,9},{9,10},{10,1... | collective-permute-start | bytes 3145736 | tf_op jit(solution)/shard_map/ppermute | solution.py:28
  83.2 48.9 %collective-permute-start.5 = (f32[1,16,128,128]{3,2,1,0:T(8,128)}, f32[1,16,128,128]{3,2,1,0:T(8,128)}, u32[]{:S(2)}, u32[]{:S(2)}) collective-permute-start(f32[1,16,128,128]{3,2,1,0:T(8,128)} %collective-permute-done.3), channel_id=1, source_target_pairs={{0,7},{1,0},{2,1},{3,2},{4,3},{5,4},{6,5},{7,6},{8,15},{9,8},{10,9... | collective-permute-start | bytes 3145736 | tf_op jit(solution)/shard_map/ppermute | solution.py:33
  94.7 39.8 %collective-permute-start.6 = (f32[1,16,128,128]{3,2,1,0:T(8,128)}, f32[1,16,128,128]{3,2,1,0:T(8,128)}, u32[]{:S(2)}, u32[]{:S(2)}) collective-permute-start(f32[1,16,128,128]{3,2,1,0:T(8,128)} %collective-permute-done.4), channel_id=1, source_target_pairs={{0,1},{1,2},{2,3},{3,4},{4,5},{5,6},{6,7},{7,0},{8,9},{9,10},{10,1... | collective-permute-start | bytes 3145736 | tf_op jit(solution)/shard_map/ppermute | solution.py:28
  122.4 2.5 copy-start.14
  124.8 1.6 copy-start.16
  161.6 1.0 copy-start
  162.7 471.1 %all-gather.14.cloned.1.call-start = ((), (), s32[]{:S(2)}) async-start(), calls=%async_computation.2 | async-start | bytes 34603008 | tf_op jit(solution)/shard_map/all_gather | solution.py:51
  189.1 7.2 %copy-start.18 = (u32[256]{0:T(256)S(1)}, u32[256]{0:T(256)}, u32[]{:S(2)}) copy-start(u32[256]{0:T(256)} %constant.252) | copy-start | bytes 3076
  190.8 10.9 %collective-permute-start.8 = (bf16[64,16,128]{2,0,1:T(8,128)(2,1)}, bf16[64,16,128]{2,0,1:T(8,128)(2,1)}, u32[]{:S(2)}, u32[]{:S(2)}) collective-permute-start(bf16[64,16,128]{2,0,1:T(8,128)(2,1)} %copy_bitcast_fusion), channel_id=1, source_target_pairs={{0,1},{1,2},{2,3},{3,4},{4,5},{5,6},{6,7},{7,8},{8,9},{9,10},{10,1... | collective-permute-start | bytes 786440 | tf_op jit(solution)/shard_map/ppermute | solution.py:44
  193.8 19.3 %collective-permute-start.7 = (bf16[64,16,128]{2,0,1:T(8,128)(2,1)S(1)}, bf16[64,16,128]{2,0,1:T(8,128)(2,1)}, u32[]{:S(2)}, u32[]{:S(2)}) collective-permute-start(bf16[64,16,128]{2,0,1:T(8,128)(2,1)S(1)} %copy_bitcast_fusion.1), channel_id=1, source_target_pairs={{0,1},{1,2},{2,3},{3,4},{4,5},{5,6},{6,7},{7,8},{8,9},{9,10},{10,1... | collective-permute-start | bytes 786440 | tf_op jit(solution)/shard_map/ppermute | solution.py:44
  196.0 8.5 %copy-start.17 = (bf16[128,16,128]{2,0,1:T(8,128)(2,1)}, bf16[128,16,128]{2,0,1:T(8,128)(2,1)S(1)}, u32[]{:S(2)}) copy-start(bf16[128,16,128]{2,0,1:T(8,128)(2,1)S(1)} %copy.84) | copy-start | bytes 1572868
  196.3 16.8 %copy-start.4 = (bf16[128,16,128]{2,0,1:T(8,128)(2,1)}, bf16[128,16,128]{2,0,1:T(8,128)(2,1)S(1)}, u32[]{:S(2)}) copy-start(bf16[128,16,128]{2,0,1:T(8,128)(2,1)S(1)} %copy.82) | copy-start | bytes 1572868
  198.2 2.0 copy-start.7
  198.8 2.9 copy-start.5
  209.9 478.3 %collective-permute-start.10 = (bf16[64,16,128]{0,2,1:T(8,128)(2,1)}, bf16[64,16,128]{0,2,1:T(8,128)(2,1)}, u32[]{:S(2)}, u32[]{:S(2)}) collective-permute-start(bf16[64,16,128]{0,2,1:T(8,128)(2,1)} %slice.107), channel_id=1, source_target_pairs={{1,0},{2,1},{3,2},{4,3},{5,4},{6,5},{7,6},{8,7},{9,8},{10,9},{11,1... | collective-permute-start | bytes 786440 | tf_op jit(solution)/shard_map/ppermute | solution.py:44
  222.6 478.2 %collective-permute-start.9 = (bf16[64,16,128]{0,2,1:T(8,128)(2,1)}, bf16[64,16,128]{0,2,1:T(8,128)(2,1)}, u32[]{:S(2)}, u32[]{:S(2)}) collective-permute-start(bf16[64,16,128]{0,2,1:T(8,128)(2,1)} %slice.108), channel_id=1, source_target_pairs={{1,0},{2,1},{3,2},{4,3},{5,4},{6,5},{7,6},{8,7},{9,8},{10,9},{11,1... | collective-permute-start | bytes 786440 | tf_op jit(solution)/shard_map/ppermute | solution.py:44
  680.6 3.4 copy-start.8
  680.6 3.4 copy-start.11
  684.4 3.9 copy-start.2
  696.3 2.5 copy-start.3
  696.3 2.5 copy-start.6
  (2 other events, 2.0 us)
Sparse Core Ops, SparseCore 0:
  13.5 70.7 all-gather.11
  162.8 237.1 all-gather.9
  402.5 231.2 all-gather.13
